TPU v7x, 128 devices: a whole 4x4x4 slice. The times are simulated.
128 devices in a mesh: frame: 4 (over x), pix: 32 (over y, z, core).
Axes of the slice: x: 4, y: 4, z: 4, core: 2. Of those that a mesh axis runs over, the one named last changes fastest.
Arguments:
- frames: bfloat16 [128, 4, 512, 512], P('frame', None, 'pix'), may hold values from -26 to 26
- prev_fg: bfloat16 [128, 4, 512, 512], P('frame', None, 'pix'), may hold values from -3 to 3
- depth_valid: int32 [128, 512, 512], P('frame', 'pix'), may hold values 0 or 1
- sketch: float32 [128, 64], replicated, may hold values from -0.5 to 0.5
- tv_weight: float32 [4], replicated, may hold values from 0.1 to 1
Outputs:
- background: bfloat16 [128, 4, 512, 512], P('frame', None, 'pix')
- foreground: bfloat16 [128, 4, 512, 512], P('frame', None, 'pix')
All inputs are finite; a program needn't handle non-finite values. No bound on the sum of `depth_valid` on one device may be relied on, other than what follows from the above.
Results may differ from a plain program's by a relative error of at most 0.012.
The roundings to bfloat16 on the way count: a program that leaves them out, or rounds other values in their place, can miss the bound.
Values may be sent and summed in bfloat16 or wider, within the bound.
A program may use at most 64 MiB of HBM per device.

v0:
```python
import jax
import jax.numpy as jnp
from jax import lax
from jax.sharding import PartitionSpec as P

POWER = 3
NSWEEP = 5
STEP_SIZE = 0.125


def shortened(shard):

    def short(part):
        return part.astype(jnp.bfloat16) if part.dtype == jnp.float32 else part

    return jax.tree.map(short, shard)


def from_behind(value, axis, steps):
    count = lax.axis_size(axis)
    leading, last = (max(0, -steps), min(count, count - steps))
    return lax.ppermute(value, axis, [(source, source + steps) for source in range(leading, last)])


def exact_dot(left, right):
    return jnp.dot(left, right, precision=lax.Precision.HIGHEST)


def mixing_matrix(gram, sketch):
    basis = sketch
    for turn in range(POWER):
        image = exact_dot(gram, basis)
        factor = jnp.linalg.cholesky(exact_dot(basis.T, image))
        basis = lax.linalg.triangular_solve(
            factor, image, left_side=False, lower=True, transpose_a=True
        )
    image = exact_dot(gram, basis)
    factor = jnp.linalg.cholesky(exact_dot(basis.T, image))
    middle = lax.linalg.triangular_solve(
        factor, exact_dot(basis.T, gram), left_side=True, lower=True
    )
    coeffs = lax.linalg.triangular_solve(
        factor, middle, left_side=True, lower=True, transpose_a=True
    )
    return exact_dot(basis, coeffs)


def pair_rows(left, right):
    return lax.dot_general(
        left, right, (((1,), (1,)), ((), ())), preferred_element_type=jnp.float32
    )


def over_frames(weights, pixels):
    return lax.dot_general(
        weights, pixels, (((0,), (0,)), ((), ())), preferred_element_type=jnp.float32
    )


def dual_update(first, second, down, across, step):
    size = jnp.sqrt(down * down + across * across)
    scale = 1.0 + step * size
    return ((first - step * down) / scale, (second - step * across) / scale)


def col_prev(field):
    return jnp.pad(field[:, :, :, :-1], ((0, 0), (0, 0), (0, 0), (1, 0)))


def col_grad(smooth, last_col):
    next_cols = jnp.pad(smooth[:, :, :, 1:], ((0, 0), (0, 0), (0, 0), (0, 1)))
    return jnp.where(last_col, 0.0, next_cols - smooth)


def local(frames, prev_fg, depth_valid, sketch, tv_weight):
    count, chans, rows, cols = frames.shape
    height = rows * lax.axis_size("pix")
    nval = chans * height * cols
    start_frame = lax.axis_index("frame") * count
    chan_ids = lax.broadcasted_iota(jnp.int32, (1, chans, 1, 1), 1)
    depth_ok = depth_valid[:, None, :, :].astype(jnp.float32)
    valid = jnp.where(chan_ids == chans - 1, depth_ok, jnp.float32(1.0))
    resid = ((frames.astype(jnp.float32) - prev_fg.astype(jnp.float32)) * valid).astype(
        jnp.bfloat16
    )
    flat = resid.reshape(count, chans * rows * cols)
    everyone = lax.all_gather(flat, "frame", axis=0, tiled=True)
    block = pair_rows(everyone, flat)
    summed = lax.psum(block, "pix")
    gram = lax.all_gather(summed, "frame", axis=1, tiled=True)
    gram = gram / nval
    mixing = mixing_matrix(gram, sketch)
    mine = lax.dynamic_slice_in_dim(mixing, start_frame, count, 1).astype(jnp.bfloat16)
    back = over_frames(mine, everyone)
    background = back.reshape(count, chans, rows, cols).astype(jnp.bfloat16)
    rounded = lax.optimization_barrier(background).astype(jnp.float32)
    source = (frames.astype(jnp.float32) - rounded) * valid
    lam = tv_weight.reshape(1, chans, 1, 1)
    step = STEP_SIZE / lam
    last_col = lax.broadcasted_iota(jnp.int32, (1, 1, 1, cols), 3) == cols - 1
    row_ids = lax.axis_index("pix") * rows + lax.broadcasted_iota(jnp.int32, (1, 1, rows, 1), 2)
    last_row = row_ids == height - 1

    def divergence(first, second):
        above = from_behind(shortened(first[:, :, -1:, :]), "pix", 1)
        prev_rows = jnp.concatenate([above, first[:, :, :-1, :]], axis=2)
        return first - prev_rows + (second - col_prev(second))

    first = jnp.zeros_like(source)
    second = jnp.zeros_like(source)
    for sweep in range(NSWEEP):
        smooth = source - lam * divergence(first, second)
        below = from_behind(shortened(smooth[:, :, :1, :]), "pix", -1)
        next_rows = jnp.concatenate([smooth[:, :, 1:, :], below], axis=2)
        down = jnp.where(last_row, 0.0, next_rows - smooth)
        across = col_grad(smooth, last_col)
        first, second = dual_update(first, second, down, across, step)
    smooth = source - lam * divergence(first, second)
    return (background, smooth.astype(jnp.bfloat16))


def solution(mesh):
    placed = (
        P("frame", None, "pix", None),
        P("frame", None, "pix", None),
        P("frame", "pix", None),
        P(),
        P(),
    )
    return jax.shard_map(
        local,
        mesh=mesh,
        in_specs=placed,
        out_specs=(P("frame", None, "pix", None), P("frame", None, "pix", None)),
        check_vma=False,
    )
```

profile of v0, /device:TPU:8, one launch (start us, length us, event | category | flops | bytes accessed | tf_op | source)
XLA Modules:
  0.0 442.0 jit_solution(11430136703876754686)
XLA Ops:
  9.7 3.6 fusion
  17.5 82.8 %all-gather.2.cloned.1.call-done = bf16[128,32768]{1,0:T(8,128)(2,1)} async-done(((bf16[32,32768]{1,0:T(8,128)(2,1)}), bf16[128,32768]{1,0:T(8,128)(2,1)}) %all-gather.2.cloned.1.call-update) | async-done | bytes 8388624 | tf_op jit(solution)/shard_map/all_gather | solution.py:87
  100.3 6.9 %fusion.61 = f32[128,32]{0,1:T(8,128)S(1)} fusion(bf16[128,32768]{1,0:T(8,128)(2,1)} %all-gather.2.cloned.1.call-done, bf16[32,32768]{1,0:T(8,128)(2,1)} %bitcast.91), kind=kOutput, calls=%fused_computation.132 | convolution fusion | flops 268435456 | bytes 10502144 | tf_op jit(solution)/shard_map/dot_general | solution.py:49
  107.2 110.5 %psum.7 = f32[128,32]{0,1:T(8,128)S(1)} all-reduce(f32[128,32]{0,1:T(8,128)S(1)} %fusion.61), channel_id=1, replica_groups=mesh['frame'=4,'pix'=32] {'pix'}, use_global_device_ids=true, to_apply=%region_0.1 | all-reduce | flops 4096 | bytes 32768 | tf_op jit(solution)/shard_map/psum | solution.py:89
  217.7 12.0 %all_gather.7 = f32[128,128]{0,1:T(8,128)S(1)} all-gather(f32[128,32]{0,1:T(8,128)S(1)} %psum.7), channel_id=1, replica_groups=mesh['frame'=4,'pix'=32] {'frame'}, dimensions={1}, use_global_device_ids=true | all-gather | bytes 81920 | tf_op jit(solution)/shard_map/all_gather | solution.py:90
  230.2 5.8 %cholesky.74 = f32[64,64]{1,0:T(8,128)S(1)} custom-call(f32[64,64]{1,0:T(8,128)S(1)} %add_multiply_fusion), custom_call_target="Cholesky" | custom-call | tf_op jit(solution)/shard_map/jit(cholesky)/cholesky | solution.py:33
  237.4 4.9 %custom-call.13 = f32[1,64,64]{1,2,0:T(8,128)S(1)} custom-call(f32[1,64,64]{2,1,0:T(8,128)S(1)} %fusion.32), custom_call_target="InvertDiagBlocksLowerTriangular" | custom-call | tf_op jit(solution)/shard_map/triangular_solve/custom-call.0 | solution.py:34
  243.0 5.8 %cholesky.85 = f32[64,64]{1,0:T(8,128)S(1)} custom-call(f32[64,64]{1,0:T(8,128)S(1)} %fusion.44), custom_call_target="Cholesky" | custom-call | tf_op jit(solution)/shard_map/jit(cholesky)/cholesky | solution.py:33
  250.2 4.9 %custom-call.14 = f32[1,64,64]{1,2,0:T(8,128)S(1)} custom-call(f32[1,64,64]{2,1,0:T(8,128)S(1)} %fusion.33), custom_call_target="InvertDiagBlocksLowerTriangular" | custom-call | tf_op jit(solution)/shard_map/triangular_solve/custom-call.0 | solution.py:34
  255.8 5.8 %cholesky.96 = f32[64,64]{1,0:T(8,128)S(1)} custom-call(f32[64,64]{1,0:T(8,128)S(1)} %fusion.42), custom_call_target="Cholesky" | custom-call | tf_op jit(solution)/shard_map/jit(cholesky)/cholesky | solution.py:33
  263.0 4.9 %custom-call.15 = f32[1,64,64]{1,2,0:T(8,128)S(1)} custom-call(f32[1,64,64]{2,1,0:T(8,128)S(1)} %fusion.34), custom_call_target="InvertDiagBlocksLowerTriangular" | custom-call | tf_op jit(solution)/shard_map/triangular_solve/custom-call.0 | solution.py:34
  268.9 5.8 %cholesky.107 = f32[64,64]{1,0:T(8,128)S(1)} custom-call(f32[64,64]{1,0:T(8,128)S(1)} %fusion.40), custom_call_target="Cholesky" | custom-call | tf_op jit(solution)/shard_map/jit(cholesky)/cholesky | solution.py:38
  276.1 4.9 %custom-call.10 = f32[1,64,64]{1,2,0:T(8,128)S(1)} custom-call(f32[1,64,64]{2,1,0:T(8,128)S(1)} %fusion.35), custom_call_target="InvertDiagBlocksLowerTriangular" | custom-call | tf_op jit(solution)/shard_map/triangular_solve | solution.py:42
  281.7 4.6 %convolution_convert_fusion = bf16[32,32768]{1,0:T(8,128)(2,1)S(1)} fusion(bf16[128,32768]{1,0:T(8,128)(2,1)} %all-gather.2.cloned.1.call-done, bf16[128,128]{0,1:T(8,128)(2,1)S(1)} %fusion.66, s32[]{:T(128)S(6)} %select_n.43), kind=kOutput, calls=%fused_computation | convolution fusion | flops 269484032 | bytes 10493956 | tf_op jit(solution)/shard_map/dot_general | solution.py:55
  287.1 3.5 multiply_subtract_fusion
  298.7 3.6 subtract_divide_fusion.8
  305.6 7.1 %collective-permute-done.2 = bf16[32,4,1,512]{3,0,2,1:T(8,128)(2,1)S(1)} collective-permute-done((bf16[32,4,1,512]{3,0,2,1:T(8,128)(2,1)S(1)}, bf16[32,4,1,512]{3,0,2,1:T(8,128)(2,1)S(1)}, u32[]{:S(2)}, u32[]{:S(2)}) %collective-permute-start.2) | collective-permute-done | bytes 131104 | tf_op jit(solution)/shard_map/ppermute | solution.py:22
  312.8 5.2 %fusion.4 = f32[32,4,16,512]{3,0,2,1:T(8,128)S(1)} fusion(f32[32,4,16,512]{3,0,2,1:T(8,128)S(1)} %get-tuple-element.17, f32[32,4,15,512]{3,0,2,1:T(8,128)S(1)} %slice.153, f32[32,4,1,512]{3,0,2,1:T(8,128)S(1)} %convert_element_type.96, f32[32,4,16,512]{3,0,2,1:T(8,128)S(1)} %get-tuple-element.16, f32[32,4,16,511]{3,0,2,1:T(8,128)S(1)} %bitcast.88, ...), kind=kLoop, calls=%fused_computation.11 | loop fusion | flops 11534336 | bytes 26206228 | tf_op jit(solution)/shard_map/sub | solution.py:112
  322.5 3.1 slice.157
  325.7 5.9 %subtract_divide_fusion.6 = (f32[32,4,16,512]{3,0,2,1:T(8,128)S(1)}, f32[32,4,16,512]{3,0,2,1:T(8,128)S(1)}) fusion(f32[32,4,16,512]{3,0,2,1:T(8,128)S(1)} %get-tuple-element.16, f32[4]{0:T(128)S(1)} %broadcast_divide_fusion, f32[32,4,16,512]{3,0,2,1:T(8,128)S(1)} %fusion.4, f32[32,4,16,511]{3,0,2,1:T(8,128)} %slice.157, ...), kind=kLoop, calls=%fused_computation.49 | loop fusion | flops 16777216 | bytes 29352480 | tf_op jit(solution)/shard_map/div | solution.py:63
  335.1 6.7 %collective-permute-done.4 = bf16[32,4,1,512]{3,0,2,1:T(8,128)(2,1)S(1)} collective-permute-done((bf16[32,4,1,512]{3,0,2,1:T(8,128)(2,1)S(1)}, bf16[32,4,1,512]{3,0,2,1:T(8,128)(2,1)S(1)}, u32[]{:S(2)}, u32[]{:S(2)}) %collective-permute-start.4) | collective-permute-done | bytes 131104 | tf_op jit(solution)/shard_map/ppermute | solution.py:22
  341.8 5.2 %fusion.8 = f32[32,4,16,512]{3,0,2,1:T(8,128)S(1)} fusion(f32[32,4,16,512]{3,0,2,1:T(8,128)S(1)} %get-tuple-element.15, f32[32,4,15,512]{3,0,2,1:T(8,128)S(1)} %slice.159, f32[32,4,1,512]{3,0,2,1:T(8,128)S(1)} %convert_element_type.98, f32[32,4,16,512]{3,0,2,1:T(8,128)S(1)} %get-tuple-element.14, f32[32,4,16,511]{3,0,2,1:T(8,128)S(1)} %bitcast.86, ...), kind=kLoop, calls=%fused_computation.17 | loop fusion | flops 11534336 | bytes 26206228 | tf_op jit(solution)/shard_map/sub | solution.py:112
  351.6 3.1 slice.163
  354.7 5.9 %subtract_divide_fusion.4 = (f32[32,4,16,512]{3,0,2,1:T(8,128)S(1)}, f32[32,4,16,512]{3,0,2,1:T(8,128)S(1)}) fusion(f32[32,4,16,512]{3,0,2,1:T(8,128)S(1)} %get-tuple-element.14, f32[4]{0:T(128)S(1)} %broadcast_divide_fusion, f32[32,4,16,512]{3,0,2,1:T(8,128)S(1)} %fusion.8, f32[32,4,16,511]{3,0,2,1:T(8,128)} %slice.163, ...), kind=kLoop, calls=%fused_computation.45 | loop fusion | flops 16777216 | bytes 29352480 | tf_op jit(solution)/shard_map/div | solution.py:63
  363.8 7.1 %collective-permute-done.6 = bf16[32,4,1,512]{3,0,2,1:T(8,128)(2,1)S(1)} collective-permute-done((bf16[32,4,1,512]{3,0,2,1:T(8,128)(2,1)S(1)}, bf16[32,4,1,512]{3,0,2,1:T(8,128)(2,1)S(1)}, u32[]{:S(2)}, u32[]{:S(2)}) %collective-permute-start.6) | collective-permute-done | bytes 131104 | tf_op jit(solution)/shard_map/ppermute | solution.py:22
  370.9 5.2 %fusion.12 = f32[32,4,16,512]{3,0,2,1:T(8,128)S(1)} fusion(f32[32,4,16,512]{3,0,2,1:T(8,128)S(1)} %get-tuple-element.13, f32[32,4,15,512]{3,0,2,1:T(8,128)S(1)} %slice.165, f32[32,4,1,512]{3,0,2,1:T(8,128)S(1)} %convert_element_type.100, f32[32,4,16,512]{3,0,2,1:T(8,128)S(1)} %get-tuple-element.12, f32[32,4,16,511]{3,0,2,1:T(8,128)S(1)} %bitcast.87, ...), kind=kLoop, calls=%fused_computation.23 | loop fusion | flops 11534336 | bytes 26206228 | tf_op jit(solution)/shard_map/sub | solution.py:112
  383.9 5.9 %subtract_divide_fusion.2 = (f32[32,4,16,512]{3,0,2,1:T(8,128)S(1)}, f32[32,4,16,512]{3,0,2,1:T(8,128)S(1)}) fusion(f32[32,4,16,512]{3,0,2,1:T(8,128)S(1)} %get-tuple-element.12, f32[4]{0:T(128)S(1)} %broadcast_divide_fusion, f32[32,4,16,512]{3,0,2,1:T(8,128)S(1)} %fusion.12, f32[32,4,16,511]{3,0,2,1:T(8,128)} %slice.169, ...), kind=kLoop, calls=%fused_computation.41 | loop fusion | flops 16777216 | bytes 29352480 | tf_op jit(solution)/shard_map/div | solution.py:63
  393.0 7.1 %collective-permute-done.8 = bf16[32,4,1,512]{3,0,2,1:T(8,128)(2,1)S(1)} collective-permute-done((bf16[32,4,1,512]{3,0,2,1:T(8,128)(2,1)S(1)}, bf16[32,4,1,512]{3,0,2,1:T(8,128)(2,1)S(1)}, u32[]{:S(2)}, u32[]{:S(2)}) %collective-permute-start.8) | collective-permute-done | bytes 131104 | tf_op jit(solution)/shard_map/ppermute | solution.py:22
  400.1 5.2 %fusion.16 = f32[32,4,16,512]{3,0,2,1:T(8,128)S(1)} fusion(f32[32,4,16,512]{3,0,2,1:T(8,128)S(1)} %get-tuple-element.11, f32[32,4,15,512]{3,0,2,1:T(8,128)S(1)} %slice.171, f32[32,4,1,512]{3,0,2,1:T(8,128)S(1)} %convert_element_type.102, f32[32,4,16,512]{3,0,2,1:T(8,128)S(1)} %get-tuple-element.10, f32[32,4,16,511]{3,0,2,1:T(8,128)S(1)} %bitcast.85, ...), kind=kLoop, calls=%fused_computation.29 | loop fusion | flops 11534336 | bytes 26206228 | tf_op jit(solution)/shard_map/sub | solution.py:112
  413.0 5.9 %subtract_divide_fusion = (f32[32,4,16,512]{3,0,2,1:T(8,128)S(1)}, f32[32,4,16,512]{3,0,2,1:T(8,128)S(1)}) fusion(f32[32,4,16,512]{3,0,2,1:T(8,128)S(1)} %get-tuple-element.10, f32[4]{0:T(128)S(1)} %broadcast_divide_fusion, f32[32,4,16,512]{3,0,2,1:T(8,128)S(1)} %fusion.16, f32[32,4,16,511]{3,0,2,1:T(8,128)} %slice.175, ...), kind=kLoop, calls=%fused_computation.37 | loop fusion | flops 16777216 | bytes 29352480 | tf_op jit(solution)/shard_map/div | solution.py:63
  422.3 5.0 %collective-permute-done.10 = bf16[32,4,1,512]{3,0,2,1:T(8,128)(2,1)S(1)} collective-permute-done((bf16[32,4,1,512]{3,0,2,1:T(8,128)(2,1)S(1)}, bf16[32,4,1,512]{3,0,2,1:T(8,128)(2,1)S(1)}, u32[]{:S(2)}, u32[]{:S(2)}) %collective-permute-start.10) | collective-permute-done | bytes 131104 | tf_op jit(solution)/shard_map/ppermute | solution.py:22
  427.3 5.1 %fusion.21 = bf16[32,4,16,512]{3,0,2,1:T(8,128)(2,1)S(1)} fusion(f32[32,4,16,512]{3,0,2,1:T(8,128)S(1)} %get-tuple-element.9, f32[32,4,15,512]{3,0,2,1:T(8,128)S(1)} %slice.177, f32[32,4,1,512]{3,0,2,1:T(8,128)S(1)} %convert_element_type.104, f32[32,4,16,512]{3,0,2,1:T(8,128)S(1)} %get-tuple-element.8, f32[32,4,16,511]{3,0,2,1:T(8,128)S(1)} %bitcast.89, ...), kind=kLoop, calls=%fused_computation.36 | loop fusion | flops 12582912 | bytes 24109076 | tf_op jit(solution)/shard_map/convert_element_type | solution.py:119
  (118 shorter events, 68.0 us)
Async XLA Ops:
  7.2 222.6 %copy-start = (f32[128,64]{0,1:T(8,128)S(1)}, f32[128,64]{0,1:T(8,128)}, u32[]{:S(2)}) copy-start(f32[128,64]{0,1:T(8,128)} %param.11) | copy-start | bytes 98308
  7.2 2.2 copy-start.2
  7.2 93.1 %all-gather.2.cloned.1.call-start = ((), (), s32[]{:S(2)}) async-start(), calls=%async_computation | async-start | bytes 10485760 | tf_op jit(solution)/shard_map/all_gather | solution.py:87
  7.2 2.5 copy-start.7
  13.3 4.2 copy-start.8
  15.5 271.5 %collective-permute-start = (bf16[32,4,1,512]{3,0,2,1:T(8,128)(2,1)}, bf16[32,4,1,512]{3,0,2,1:T(8,128)(2,1)S(1)}, u32[]{:S(2)}, u32[]{:S(2)}) collective-permute-start(bf16[32,4,1,512]{3,0,2,1:T(8,128)(2,1)} %convert_element_type.94), channel_id=1, source_target_pairs={{0,1},{1,2},{2,3},{3,4},{4,5},{5,6},{6,7},{7,8},{8,9},{9,10},{10,1... | collective-permute-start | bytes 393224 | tf_op jit(solution)/shard_map/ppermute | solution.py:22
  287.0 3.5 copy-start.3
  290.5 1.9 copy-start.5
  292.5 5.3 %collective-permute-start.1 = (bf16[32,4,1,512]{3,0,2,1:T(8,128)(2,1)S(1)}, bf16[32,4,1,512]{3,0,2,1:T(8,128)(2,1)S(1)}, u32[]{:S(2)}, u32[]{:S(2)}) collective-permute-start(bf16[32,4,1,512]{3,0,2,1:T(8,128)(2,1)S(1)} %slice.198), channel_id=1, source_target_pairs={{1,0},{2,1},{3,2},{4,3},{5,4},{6,5},{7,6},{8,7},{9,8},{10,9},{11,1... | collective-permute-start | bytes 393224 | tf_op jit(solution)/shard_map/ppermute | solution.py:22
  294.4 2.2 copy-start.6
  296.6 2.1 slice-start
  302.4 10.4 %copy-start.4 = (bf16[4,8,64,512]{3,2,1,0:T(8,128)(2,1)S(1)}, bf16[4,8,64,512]{3,2,1,0:T(8,128)(2,1)}, u32[]{:S(2)}) copy-start(bf16[4,8,64,512]{3,2,1,0:T(8,128)(2,1)} %copy-done.3) | copy-start | bytes 6291460
  302.4 10.4 %collective-permute-start.2 = (bf16[32,4,1,512]{3,0,2,1:T(8,128)(2,1)S(1)}, bf16[32,4,1,512]{3,0,2,1:T(8,128)(2,1)S(1)}, u32[]{:S(2)}, u32[]{:S(2)}) collective-permute-start(bf16[32,4,1,512]{3,0,2,1:T(8,128)(2,1)S(1)} %slice.197), channel_id=1, source_target_pairs={{0,1},{1,2},{2,3},{3,4},{4,5},{5,6},{6,7},{7,8},{8,9},{9,10},{10,1... | collective-permute-start | bytes 393224 | tf_op jit(solution)/shard_map/ppermute | solution.py:22
  318.0 7.6 %collective-permute-start.3 = (bf16[32,4,1,512]{3,0,2,1:T(8,128)(2,1)S(1)}, bf16[32,4,1,512]{3,0,2,1:T(8,128)(2,1)S(1)}, u32[]{:S(2)}, u32[]{:S(2)}) collective-permute-start(bf16[32,4,1,512]{3,0,2,1:T(8,128)(2,1)S(1)} %slice.196), channel_id=1, source_target_pairs={{1,0},{2,1},{3,2},{4,3},{5,4},{6,5},{7,6},{8,7},{9,8},{10,9},{11,1... | collective-permute-start | bytes 393224 | tf_op jit(solution)/shard_map/ppermute | solution.py:22
  331.6 10.2 %collective-permute-start.4 = (bf16[32,4,1,512]{3,0,2,1:T(8,128)(2,1)S(1)}, bf16[32,4,1,512]{3,0,2,1:T(8,128)(2,1)S(1)}, u32[]{:S(2)}, u32[]{:S(2)}) collective-permute-start(bf16[32,4,1,512]{3,0,2,1:T(8,128)(2,1)S(1)} %slice.195), channel_id=1, source_target_pairs={{0,1},{1,2},{2,3},{3,4},{4,5},{5,6},{6,7},{7,8},{8,9},{9,10},{10,1... | collective-permute-start | bytes 393224 | tf_op jit(solution)/shard_map/ppermute | solution.py:22
  347.1 7.6 %collective-permute-start.5 = (bf16[32,4,1,512]{3,0,2,1:T(8,128)(2,1)S(1)}, bf16[32,4,1,512]{3,0,2,1:T(8,128)(2,1)S(1)}, u32[]{:S(2)}, u32[]{:S(2)}) collective-permute-start(bf16[32,4,1,512]{3,0,2,1:T(8,128)(2,1)S(1)} %slice.194), channel_id=1, source_target_pairs={{1,0},{2,1},{3,2},{4,3},{5,4},{6,5},{7,6},{8,7},{9,8},{10,9},{11,1... | collective-permute-start | bytes 393224 | tf_op jit(solution)/shard_map/ppermute | solution.py:22
  360.6 10.2 %collective-permute-start.6 = (bf16[32,4,1,512]{3,0,2,1:T(8,128)(2,1)S(1)}, bf16[32,4,1,512]{3,0,2,1:T(8,128)(2,1)S(1)}, u32[]{:S(2)}, u32[]{:S(2)}) collective-permute-start(bf16[32,4,1,512]{3,0,2,1:T(8,128)(2,1)S(1)} %slice.193), channel_id=1, source_target_pairs={{0,1},{1,2},{2,3},{3,4},{4,5},{5,6},{6,7},{7,8},{8,9},{9,10},{10,1... | collective-permute-start | bytes 393224 | tf_op jit(solution)/shard_map/ppermute | solution.py:22
  376.1 7.8 %collective-permute-start.7 = (bf16[32,4,1,512]{3,0,2,1:T(8,128)(2,1)S(1)}, bf16[32,4,1,512]{3,0,2,1:T(8,128)(2,1)S(1)}, u32[]{:S(2)}, u32[]{:S(2)}) collective-permute-start(bf16[32,4,1,512]{3,0,2,1:T(8,128)(2,1)S(1)} %slice.192), channel_id=1, source_target_pairs={{1,0},{2,1},{3,2},{4,3},{5,4},{6,5},{7,6},{8,7},{9,8},{10,9},{11,1... | collective-permute-start | bytes 393224 | tf_op jit(solution)/shard_map/ppermute | solution.py:22
  389.8 10.2 %collective-permute-start.8 = (bf16[32,4,1,512]{3,0,2,1:T(8,128)(2,1)S(1)}, bf16[32,4,1,512]{3,0,2,1:T(8,128)(2,1)S(1)}, u32[]{:S(2)}, u32[]{:S(2)}) collective-permute-start(bf16[32,4,1,512]{3,0,2,1:T(8,128)(2,1)S(1)} %slice.191), channel_id=1, source_target_pairs={{0,1},{1,2},{2,3},{3,4},{4,5},{5,6},{6,7},{7,8},{8,9},{9,10},{10,1... | collective-permute-start | bytes 393224 | tf_op jit(solution)/shard_map/ppermute | solution.py:22
  405.4 7.6 %collective-permute-start.9 = (bf16[32,4,1,512]{3,0,2,1:T(8,128)(2,1)S(1)}, bf16[32,4,1,512]{3,0,2,1:T(8,128)(2,1)S(1)}, u32[]{:S(2)}, u32[]{:S(2)}) collective-permute-start(bf16[32,4,1,512]{3,0,2,1:T(8,128)(2,1)S(1)} %slice.190), channel_id=1, source_target_pairs={{1,0},{2,1},{3,2},{4,3},{5,4},{6,5},{7,6},{8,7},{9,8},{10,9},{11,1... | collective-permute-start | bytes 393224 | tf_op jit(solution)/shard_map/ppermute | solution.py:22
  418.9 8.4 %collective-permute-start.10 = (bf16[32,4,1,512]{3,0,2,1:T(8,128)(2,1)S(1)}, bf16[32,4,1,512]{3,0,2,1:T(8,128)(2,1)S(1)}, u32[]{:S(2)}, u32[]{:S(2)}) collective-permute-start(bf16[32,4,1,512]{3,0,2,1:T(8,128)(2,1)S(1)} %slice.189), channel_id=1, source_target_pairs={{0,1},{1,2},{2,3},{3,4},{4,5},{5,6},{6,7},{7,8},{8,9},{9,10},{10,1... | collective-permute-start | bytes 393224 | tf_op jit(solution)/shard_map/ppermute | solution.py:22
  427.3 7.6 %copy-start.1 = (f32[128,64]{0,1:T(8,128)S(1)}, f32[128,64]{0,1:T(8,128)}, u32[]{:S(2)}) copy-start(f32[128,64]{0,1:T(8,128)} %param.11) | copy-start | bytes 98308
Sparse Core Ops, SparseCore 0:
  15.0 85.3 all-gather.1
where the time goes:
time: 448 us; the launch traced here: 442 us
  blocking collectives  122 us (27%)
  waiting for transfers between devices  116 us (26%)
  other arithmetic  110 us (25%)
  local copies, waits for them, and re-layouts  39.3 us (9%)
  starting transfers between devices  24.5 us (5%)
  between operations  15 us (3%)
  matrix products  14.7 us (3%)
    psum x1, blocking collectives, local(): summed = lax.psum(block, 'pix')  110 us
    all_gather x1, waiting for transfers between devices, local(): everyone = lax.all_gather(flat, 'frame', axis=0, tiled=True)  82.8 us
    ppermute x11, waiting for transfers between devices, from_behind(): lax.ppermute(value, axis, [(source, source + steps) for source in range(l...  33 us
    div x5, other arithmetic, dual_update(): return ((first - step * down) / scale, (second - step * across) / scale)  27.1 us
    another operation x12, other arithmetic, mixing_matrix(): factor = jnp.linalg.cholesky(exact_dot(basis.T, image))  26.1 us
    ppermute x11, starting transfers between devices, from_behind(): lax.ppermute(value, axis, [(source, source + steps) for source in range(l...  24.5 us
    sub x5, other arithmetic, local(): smooth = source - lam * divergence(first, second)  24.3 us
    another operation x6, other arithmetic, mixing_matrix(): lax.linalg.triangular_solve(factor, image, left_side=False, lower=True, t...  16.6 us
  transfers between devices with their start and end apart: 12, of which 6 were waited for; matrix products, arithmetic and copies ran while one was open for 21% of the time, Pallas kernels for 0%

commit v1 on v0

--- a/solution.py
+++ b/solution.py
@@ -86,7 +86,11 @@
     flat = resid.reshape(count, chans * rows * cols)
     everyone = lax.all_gather(flat, "frame", axis=0, tiled=True)
     block = pair_rows(everyone, flat)
-    summed = lax.psum(block, "pix")
+    n_dev = lax.axis_size("pix")
+    summed, far = (block, 1)
+    while far < n_dev:
+        summed = summed + lax.ppermute(summed, "pix", [(i, i ^ far) for i in range(n_dev)])
+        far = 2 * far
     gram = lax.all_gather(summed, "frame", axis=1, tiled=True)
     gram = gram / nval
     mixing = mixing_matrix(gram, sketch)

time: 448 us -> 351 us (0.78)
  blocking collectives: 122 us -> 12.1 us
  starting transfers between devices: 24.5 us -> 31.4 us
  waiting for transfers between devices: 116 us -> 121 us
    psum x1 -> x0, blocking collectives: 110 us -> none  [local(): summed = lax.psum(block, 'pix')]
    ppermute x0 -> x5, waiting for transfers between devices: none -> 10.1 us  [local(): lax.ppermute(summed, 'pix', [(i, i ^ far) for i in range(n_dev)])]
    ppermute x11, waiting for transfers between devices: 33 us -> 25.7 us  [from_behind(): lax.ppermute(value, axis, [(source, source + steps) for source in range(l...]
    ppermute x0 -> x5, starting transfers between devices: none -> 6.95 us  [local(): lax.ppermute(summed, 'pix', [(i, i ^ far) for i in range(n_dev)])]
  transfers between devices with their start and end apart: 12 -> 17, of which waited for: 6 -> 10; matrix products, arithmetic and copies ran while one was open for 21% -> 25% of each run, Pallas kernels for 0% -> 0%
where the time goes in v1:
time: 351 us; the launch traced here: 344 us
  waiting for transfers between devices  121 us (34%)
  other arithmetic  110 us (31%)
  local copies, waits for them, and re-layouts  39.5 us (11%)
  starting transfers between devices  31.4 us (9%)
  between operations  15 us (4%)
  matrix products  14.7 us (4%)
  blocking collectives  12.1 us (3%)
    all_gather x1, waiting for transfers between devices, local(): everyone = lax.all_gather(flat, 'frame', axis=0, tiled=True)  85.5 us
    div x5, other arithmetic, dual_update(): return ((first - step * down) / scale, (second - step * across) / scale)  27.1 us
    another operation x12, other arithmetic, mixing_matrix(): factor = jnp.linalg.cholesky(exact_dot(basis.T, image))  26.1 us
    ppermute x11, waiting for transfers between devices, from_behind(): lax.ppermute(value, axis, [(source, source + steps) for source in range(l...  25.7 us
    ppermute x11, starting transfers between devices, from_behind(): lax.ppermute(value, axis, [(source, source + steps) for source in range(l...  24.5 us
    sub x5, other arithmetic, local(): smooth = source - lam * divergence(first, second)  24.3 us
    another operation x6, other arithmetic, mixing_matrix(): lax.linalg.triangular_solve(factor, image, left_side=False, lower=True, t...  16.6 us
    slice x5, local copies, waits for them, and re-layouts, col_grad(): next_cols = jnp.pad(smooth[:, :, :, 1:], ((0, 0), (0, 0), (0, 0), (0, 1)))  13.5 us
  transfers between devices with their start and end apart: 17, of which 10 were waited for; matrix products, arithmetic and copies ran while one was open for 25% of the time, Pallas kernels for 0%

profile of v1, /device:TPU:8, one launch (start us, length us, event | category | flops | bytes accessed | tf_op | source)
XLA Modules:
  0.0 344.2 jit_solution(17491802390838344083)
XLA Ops:
  9.7 3.6 %fusion = bf16[32,4,16,512]{3,0,2,1:T(8,128)(2,1)S(1)} fusion(bf16[32,4,16,512]{3,2,1,0:T(8,128)(2,1)S(1)} %copy-done.7, f32[32,16,512]{2,0,1:T(8,128)S(1)} %copy.22, pred[4]{0:T(512)(128)(4,1)S(1)} %iota_compare_fusion.3, bf16[32,4,16,512]{3,2,1,0:T(8,128)(2,1)S(1)} %copy-done.2), kind=kLoop, calls=%fused_computation.5 | loop fusion | flops 6291456 | bytes 7340036 | tf_op jit(solution)/shard_map/convert_element_type | solution.py:83
  14.9 85.5 %all-gather.2.cloned.1.call-done = bf16[128,32768]{1,0:T(8,128)(2,1)} async-done(((bf16[32,32768]{1,0:T(8,128)(2,1)}), bf16[128,32768]{1,0:T(8,128)(2,1)}) %all-gather.2.cloned.1.call-update) | async-done | bytes 8388624 | tf_op jit(solution)/shard_map/all_gather | solution.py:87
  100.3 6.9 %fusion.61 = f32[128,32]{0,1:T(8,128)S(1)} fusion(bf16[128,32768]{1,0:T(8,128)(2,1)} %all-gather.2.cloned.1.call-done, bf16[32,32768]{1,0:T(8,128)(2,1)} %bitcast.91), kind=kOutput, calls=%fused_computation.132 | convolution fusion | flops 268435456 | bytes 10502144 | tf_op jit(solution)/shard_map/dot_general | solution.py:49
  112.2 3.1 collective-permute-start.2
  118.0 3.7 %collective-permute-done.3 = f32[128,32]{0,1:T(8,128)S(1)} collective-permute-done((f32[128,32]{0,1:T(8,128)S(1)}, f32[128,32]{0,1:T(8,128)S(1)}, u32[]{:S(2)}, u32[]{:S(2)}) %collective-permute-start.3) | collective-permute-done | bytes 16416 | tf_op jit(solution)/shard_map/ppermute | solution.py:92
  127.0 12.1 %all_gather.7 = f32[128,128]{0,1:T(8,128)S(1)} all-gather(f32[128,32]{0,1:T(8,128)S(1)} %add.117), channel_id=1, replica_groups=mesh['frame'=4,'pix'=32] {'frame'}, dimensions={1}, use_global_device_ids=true | all-gather | bytes 81920 | tf_op jit(solution)/shard_map/all_gather | solution.py:94
  139.5 5.8 %cholesky.74 = f32[64,64]{1,0:T(8,128)S(1)} custom-call(f32[64,64]{1,0:T(8,128)S(1)} %add_multiply_fusion), custom_call_target="Cholesky" | custom-call | tf_op jit(solution)/shard_map/jit(cholesky)/cholesky | solution.py:33
  146.7 4.9 %custom-call.13 = f32[1,64,64]{1,2,0:T(8,128)S(1)} custom-call(f32[1,64,64]{2,1,0:T(8,128)S(1)} %fusion.32), custom_call_target="InvertDiagBlocksLowerTriangular" | custom-call | tf_op jit(solution)/shard_map/triangular_solve/custom-call.0 | solution.py:34
  152.4 5.8 %cholesky.85 = f32[64,64]{1,0:T(8,128)S(1)} custom-call(f32[64,64]{1,0:T(8,128)S(1)} %fusion.44), custom_call_target="Cholesky" | custom-call | tf_op jit(solution)/shard_map/jit(cholesky)/cholesky | solution.py:33
  159.5 4.9 %custom-call.14 = f32[1,64,64]{1,2,0:T(8,128)S(1)} custom-call(f32[1,64,64]{2,1,0:T(8,128)S(1)} %fusion.33), custom_call_target="InvertDiagBlocksLowerTriangular" | custom-call | tf_op jit(solution)/shard_map/triangular_solve/custom-call.0 | solution.py:34
  165.2 5.8 %cholesky.96 = f32[64,64]{1,0:T(8,128)S(1)} custom-call(f32[64,64]{1,0:T(8,128)S(1)} %fusion.42), custom_call_target="Cholesky" | custom-call | tf_op jit(solution)/shard_map/jit(cholesky)/cholesky | solution.py:33
  172.4 4.9 %custom-call.15 = f32[1,64,64]{1,2,0:T(8,128)S(1)} custom-call(f32[1,64,64]{2,1,0:T(8,128)S(1)} %fusion.34), custom_call_target="InvertDiagBlocksLowerTriangular" | custom-call | tf_op jit(solution)/shard_map/triangular_solve/custom-call.0 | solution.py:34
  178.2 5.8 %cholesky.107 = f32[64,64]{1,0:T(8,128)S(1)} custom-call(f32[64,64]{1,0:T(8,128)S(1)} %fusion.40), custom_call_target="Cholesky" | custom-call | tf_op jit(solution)/shard_map/jit(cholesky)/cholesky | solution.py:38
  185.4 4.9 %custom-call.10 = f32[1,64,64]{1,2,0:T(8,128)S(1)} custom-call(f32[1,64,64]{2,1,0:T(8,128)S(1)} %fusion.35), custom_call_target="InvertDiagBlocksLowerTriangular" | custom-call | tf_op jit(solution)/shard_map/triangular_solve | solution.py:42
  191.1 4.6 %convolution_convert_fusion = bf16[32,32768]{1,0:T(8,128)(2,1)S(1)} fusion(bf16[128,32768]{1,0:T(8,128)(2,1)} %all-gather.2.cloned.1.call-done, bf16[128,128]{0,1:T(8,128)(2,1)S(1)} %fusion.66, s32[]{:T(128)S(6)} %select_n.43), kind=kOutput, calls=%fused_computation | convolution fusion | flops 269484032 | bytes 10493956 | tf_op jit(solution)/shard_map/dot_general | solution.py:55
  196.4 3.5 %multiply_subtract_fusion = f32[32,4,16,512]{3,0,2,1:T(8,128)S(1)} fusion(f32[512]{0:T(512)S(1)} %pad_subtract_fusion, bf16[32,4,1,512]{3,0,2,1:T(8,128)(2,1)S(1)} %collective-permute-done.5, f32[4]{0:T(128)S(1)} %copy-done.8, f32[32,16,512]{2,0,1:T(8,128)S(1)} %copy.22, pred[4]{0:T(512)(128)(4,1)S(1)} %iota_compare_fusion.3, ...), kind=kLoop, calls=%fused_computation.57 | loop fusion | flops 10485760 | bytes 9570324 | tf_op jit(solution)/shard_map/sub | solution.py:116
  208.1 3.6 %subtract_divide_fusion.8 = (f32[32,4,16,512]{3,0,2,1:T(8,128)S(1)}, f32[32,4,16,512]{3,0,2,1:T(8,128)S(1)}) fusion(f32[4]{0:T(128)S(1)} %broadcast_divide_fusion, f32[32,4,16,512]{3,0,2,1:T(8,128)S(1)} %copy-done.6, f32[32,4,16,511]{3,0,2,1:T(8,128)S(1)} %slice.151, pred[512]{0:T(512)(128)(4,1)S(1)} %iota_compare_fusion.2, ...), kind=kLoop, calls=%fused_computation.53 | loop fusion | flops 16777216 | bytes 20963872 | tf_op jit(solution)/shard_map/div | solution.py:63
  215.0 5.3 %collective-permute-done.7 = bf16[32,4,1,512]{3,0,2,1:T(8,128)(2,1)S(1)} collective-permute-done((bf16[32,4,1,512]{3,0,2,1:T(8,128)(2,1)S(1)}, bf16[32,4,1,512]{3,0,2,1:T(8,128)(2,1)S(1)}, u32[]{:S(2)}, u32[]{:S(2)}) %collective-permute-start.7) | collective-permute-done | bytes 131104 | tf_op jit(solution)/shard_map/ppermute | solution.py:22
  220.3 5.2 %fusion.4 = f32[32,4,16,512]{3,0,2,1:T(8,128)S(1)} fusion(f32[32,4,16,512]{3,0,2,1:T(8,128)S(1)} %get-tuple-element.17, f32[32,4,15,512]{3,0,2,1:T(8,128)S(1)} %slice.153, f32[32,4,1,512]{3,0,2,1:T(8,128)S(1)} %convert_element_type.96, f32[32,4,16,512]{3,0,2,1:T(8,128)S(1)} %get-tuple-element.16, f32[32,4,16,511]{3,0,2,1:T(8,128)S(1)} %bitcast.88, ...), kind=kLoop, calls=%fused_computation.11 | loop fusion | flops 11534336 | bytes 26206228 | tf_op jit(solution)/shard_map/sub | solution.py:116
  230.1 3.1 slice.157
  233.2 5.9 %subtract_divide_fusion.6 = (f32[32,4,16,512]{3,0,2,1:T(8,128)S(1)}, f32[32,4,16,512]{3,0,2,1:T(8,128)S(1)}) fusion(f32[32,4,16,512]{3,0,2,1:T(8,128)S(1)} %get-tuple-element.16, f32[4]{0:T(128)S(1)} %broadcast_divide_fusion, f32[32,4,16,512]{3,0,2,1:T(8,128)S(1)} %fusion.4, f32[32,4,16,511]{3,0,2,1:T(8,128)} %slice.157, ...), kind=kLoop, calls=%fused_computation.49 | loop fusion | flops 16777216 | bytes 29352480 | tf_op jit(solution)/shard_map/div | solution.py:63
  242.7 4.8 %collective-permute-done.9 = bf16[32,4,1,512]{3,0,2,1:T(8,128)(2,1)S(1)} collective-permute-done((bf16[32,4,1,512]{3,0,2,1:T(8,128)(2,1)S(1)}, bf16[32,4,1,512]{3,0,2,1:T(8,128)(2,1)S(1)}, u32[]{:S(2)}, u32[]{:S(2)}) %collective-permute-start.9) | collective-permute-done | bytes 131104 | tf_op jit(solution)/shard_map/ppermute | solution.py:22
  247.6 5.2 %fusion.8 = f32[32,4,16,512]{3,0,2,1:T(8,128)S(1)} fusion(f32[32,4,16,512]{3,0,2,1:T(8,128)S(1)} %get-tuple-element.15, f32[32,4,15,512]{3,0,2,1:T(8,128)S(1)} %slice.159, f32[32,4,1,512]{3,0,2,1:T(8,128)S(1)} %convert_element_type.98, f32[32,4,16,512]{3,0,2,1:T(8,128)S(1)} %get-tuple-element.14, f32[32,4,16,511]{3,0,2,1:T(8,128)S(1)} %bitcast.86, ...), kind=kLoop, calls=%fused_computation.17 | loop fusion | flops 11534336 | bytes 26206228 | tf_op jit(solution)/shard_map/sub | solution.py:116
  260.5 5.9 %subtract_divide_fusion.4 = (f32[32,4,16,512]{3,0,2,1:T(8,128)S(1)}, f32[32,4,16,512]{3,0,2,1:T(8,128)S(1)}) fusion(f32[32,4,16,512]{3,0,2,1:T(8,128)S(1)} %get-tuple-element.14, f32[4]{0:T(128)S(1)} %broadcast_divide_fusion, f32[32,4,16,512]{3,0,2,1:T(8,128)S(1)} %fusion.8, f32[32,4,16,511]{3,0,2,1:T(8,128)} %slice.163, ...), kind=kLoop, calls=%fused_computation.45 | loop fusion | flops 16777216 | bytes 29352480 | tf_op jit(solution)/shard_map/div | solution.py:63
  269.5 5.3 %collective-permute-done.11 = bf16[32,4,1,512]{3,0,2,1:T(8,128)(2,1)S(1)} collective-permute-done((bf16[32,4,1,512]{3,0,2,1:T(8,128)(2,1)S(1)}, bf16[32,4,1,512]{3,0,2,1:T(8,128)(2,1)S(1)}, u32[]{:S(2)}, u32[]{:S(2)}) %collective-permute-start.11) | collective-permute-done | bytes 131104 | tf_op jit(solution)/shard_map/ppermute | solution.py:22
  274.8 5.2 %fusion.12 = f32[32,4,16,512]{3,0,2,1:T(8,128)S(1)} fusion(f32[32,4,16,512]{3,0,2,1:T(8,128)S(1)} %get-tuple-element.13, f32[32,4,15,512]{3,0,2,1:T(8,128)S(1)} %slice.165, f32[32,4,1,512]{3,0,2,1:T(8,128)S(1)} %convert_element_type.100, f32[32,4,16,512]{3,0,2,1:T(8,128)S(1)} %get-tuple-element.12, f32[32,4,16,511]{3,0,2,1:T(8,128)S(1)} %bitcast.87, ...), kind=kLoop, calls=%fused_computation.23 | loop fusion | flops 11534336 | bytes 26206228 | tf_op jit(solution)/shard_map/sub | solution.py:116
  287.9 5.9 %subtract_divide_fusion.2 = (f32[32,4,16,512]{3,0,2,1:T(8,128)S(1)}, f32[32,4,16,512]{3,0,2,1:T(8,128)S(1)}) fusion(f32[32,4,16,512]{3,0,2,1:T(8,128)S(1)} %get-tuple-element.12, f32[4]{0:T(128)S(1)} %broadcast_divide_fusion, f32[32,4,16,512]{3,0,2,1:T(8,128)S(1)} %fusion.12, f32[32,4,16,511]{3,0,2,1:T(8,128)} %slice.169, ...), kind=kLoop, calls=%fused_computation.41 | loop fusion | flops 16777216 | bytes 29352480 | tf_op jit(solution)/shard_map/div | solution.py:63
  297.0 5.3 %collective-permute-done.13 = bf16[32,4,1,512]{3,0,2,1:T(8,128)(2,1)S(1)} collective-permute-done((bf16[32,4,1,512]{3,0,2,1:T(8,128)(2,1)S(1)}, bf16[32,4,1,512]{3,0,2,1:T(8,128)(2,1)S(1)}, u32[]{:S(2)}, u32[]{:S(2)}) %collective-permute-start.13) | collective-permute-done | bytes 131104 | tf_op jit(solution)/shard_map/ppermute | solution.py:22
  302.3 5.2 %fusion.16 = f32[32,4,16,512]{3,0,2,1:T(8,128)S(1)} fusion(f32[32,4,16,512]{3,0,2,1:T(8,128)S(1)} %get-tuple-element.11, f32[32,4,15,512]{3,0,2,1:T(8,128)S(1)} %slice.171, f32[32,4,1,512]{3,0,2,1:T(8,128)S(1)} %convert_element_type.102, f32[32,4,16,512]{3,0,2,1:T(8,128)S(1)} %get-tuple-element.10, f32[32,4,16,511]{3,0,2,1:T(8,128)S(1)} %bitcast.85, ...), kind=kLoop, calls=%fused_computation.29 | loop fusion | flops 11534336 | bytes 26206228 | tf_op jit(solution)/shard_map/sub | solution.py:116
  315.2 5.9 %subtract_divide_fusion = (f32[32,4,16,512]{3,0,2,1:T(8,128)S(1)}, f32[32,4,16,512]{3,0,2,1:T(8,128)S(1)}) fusion(f32[32,4,16,512]{3,0,2,1:T(8,128)S(1)} %get-tuple-element.10, f32[4]{0:T(128)S(1)} %broadcast_divide_fusion, f32[32,4,16,512]{3,0,2,1:T(8,128)S(1)} %fusion.16, f32[32,4,16,511]{3,0,2,1:T(8,128)} %slice.175, ...), kind=kLoop, calls=%fused_computation.37 | loop fusion | flops 16777216 | bytes 29352480 | tf_op jit(solution)/shard_map/div | solution.py:63
  324.5 5.0 %collective-permute-done.15 = bf16[32,4,1,512]{3,0,2,1:T(8,128)(2,1)S(1)} collective-permute-done((bf16[32,4,1,512]{3,0,2,1:T(8,128)(2,1)S(1)}, bf16[32,4,1,512]{3,0,2,1:T(8,128)(2,1)S(1)}, u32[]{:S(2)}, u32[]{:S(2)}) %collective-permute-start.15) | collective-permute-done | bytes 131104 | tf_op jit(solution)/shard_map/ppermute | solution.py:22
  329.5 5.1 %fusion.21 = bf16[32,4,16,512]{3,0,2,1:T(8,128)(2,1)S(1)} fusion(f32[32,4,16,512]{3,0,2,1:T(8,128)S(1)} %get-tuple-element.9, f32[32,4,15,512]{3,0,2,1:T(8,128)S(1)} %slice.177, f32[32,4,1,512]{3,0,2,1:T(8,128)S(1)} %convert_element_type.104, f32[32,4,16,512]{3,0,2,1:T(8,128)S(1)} %get-tuple-element.8, f32[32,4,16,511]{3,0,2,1:T(8,128)S(1)} %bitcast.89, ...), kind=kLoop, calls=%fused_computation.36 | loop fusion | flops 12582912 | bytes 24109076 | tf_op jit(solution)/shard_map/convert_element_type | solution.py:123
  (132 shorter events, 81.5 us)
Async XLA Ops:
  7.2 131.9 %copy-start = (f32[128,64]{0,1:T(8,128)S(1)}, f32[128,64]{0,1:T(8,128)}, u32[]{:S(2)}) copy-start(f32[128,64]{0,1:T(8,128)} %param.11) | copy-start | bytes 98308
  7.2 2.2 copy-start.2
  7.2 93.1 %all-gather.2.cloned.1.call-start = ((), (), s32[]{:S(2)}) async-start(), calls=%async_computation | async-start | bytes 10485760 | tf_op jit(solution)/shard_map/all_gather | solution.py:87
  7.2 2.5 copy-start.7
  14.8 103.2 %copy-start.8 = (f32[4]{0:T(128)S(1)}, f32[4]{0:T(128)}, u32[]{:S(2)}) copy-start(f32[4]{0:T(128)} %param.12) | copy-start | bytes 52
  107.2 1.2 collective-permute-start
  108.4 3.7 %collective-permute-start.1 = (f32[128,32]{0,1:T(8,128)S(1)}, f32[128,32]{0,1:T(8,128)S(1)}, u32[]{:S(2)}, u32[]{:S(2)}) collective-permute-start(f32[128,32]{0,1:T(8,128)S(1)} %add.113), channel_id=1, source_target_pairs={{0,2},{1,3},{2,0},{3,1},{4,6},{5,7},{6,4},{7,5},{8,10},{9,11},{10,... | collective-permute-start | bytes 49160 | tf_op jit(solution)/shard_map/ppermute | solution.py:92
  112.2 5.7 %collective-permute-start.2 = (f32[128,32]{0,1:T(8,128)S(1)}, f32[128,32]{0,1:T(8,128)S(1)}, u32[]{:S(2)}, u32[]{:S(2)}) collective-permute-start(f32[128,32]{0,1:T(8,128)S(1)} %add.114), channel_id=1, source_target_pairs={{0,4},{1,5},{2,6},{3,7},{4,0},{5,1},{6,2},{7,3},{8,12},{9,13},{10,... | collective-permute-start | bytes 49160 | tf_op jit(solution)/shard_map/ppermute | solution.py:92
  116.0 80.4 %collective-permute-start.5 = (bf16[32,4,1,512]{3,0,2,1:T(8,128)(2,1)}, bf16[32,4,1,512]{3,0,2,1:T(8,128)(2,1)S(1)}, u32[]{:S(2)}, u32[]{:S(2)}) collective-permute-start(bf16[32,4,1,512]{3,0,2,1:T(8,128)(2,1)} %convert_element_type.94), channel_id=1, source_target_pairs={{0,1},{1,2},{2,3},{3,4},{4,5},{5,6},{6,7},{7,8},{8,9},{9,10},{10,1... | collective-permute-start | bytes 393224 | tf_op jit(solution)/shard_map/ppermute | solution.py:22
  117.9 3.8 %collective-permute-start.3 = (f32[128,32]{0,1:T(8,128)S(1)}, f32[128,32]{0,1:T(8,128)S(1)}, u32[]{:S(2)}, u32[]{:S(2)}) collective-permute-start(f32[128,32]{0,1:T(8,128)S(1)} %add.115), channel_id=1, source_target_pairs={{0,8},{1,9},{2,10},{3,11},{4,12},{5,13},{6,14},{7,15},{8,0},{9,1},... | collective-permute-start | bytes 49160 | tf_op jit(solution)/shard_map/ppermute | solution.py:92
  121.8 5.2 %collective-permute-start.4 = (f32[128,32]{0,1:T(8,128)S(1)}, f32[128,32]{0,1:T(8,128)S(1)}, u32[]{:S(2)}, u32[]{:S(2)}) collective-permute-start(f32[128,32]{0,1:T(8,128)S(1)} %add.116), channel_id=1, source_target_pairs={{0,16},{1,17},{2,18},{3,19},{4,20},{5,21},{6,22},{7,23},{8,24},{9,... | collective-permute-start | bytes 49160 | tf_op jit(solution)/shard_map/ppermute | solution.py:92
  196.4 3.5 %copy-start.3 = (bf16[4,8,64,512]{3,2,1,0:T(8,128)(2,1)}, bf16[4,8,64,512]{3,2,1,0:T(8,128)(2,1)S(1)}, u32[]{:S(2)}) copy-start(bf16[4,8,64,512]{3,2,1,0:T(8,128)(2,1)S(1)} %copy.31) | copy-start | bytes 6291460
  199.9 2.0 copy-start.5
  201.8 5.3 %collective-permute-start.6 = (bf16[32,4,1,512]{3,0,2,1:T(8,128)(2,1)S(1)}, bf16[32,4,1,512]{3,0,2,1:T(8,128)(2,1)S(1)}, u32[]{:S(2)}, u32[]{:S(2)}) collective-permute-start(bf16[32,4,1,512]{3,0,2,1:T(8,128)(2,1)S(1)} %slice.198), channel_id=1, source_target_pairs={{1,0},{2,1},{3,2},{4,3},{5,4},{6,5},{7,6},{8,7},{9,8},{10,9},{11,1... | collective-permute-start | bytes 393224 | tf_op jit(solution)/shard_map/ppermute | solution.py:22
  203.8 2.2 copy-start.6
  206.0 2.1 slice-start
  211.7 8.6 %copy-start.4 = (bf16[4,8,64,512]{3,2,1,0:T(8,128)(2,1)S(1)}, bf16[4,8,64,512]{3,2,1,0:T(8,128)(2,1)}, u32[]{:S(2)}) copy-start(bf16[4,8,64,512]{3,2,1,0:T(8,128)(2,1)} %copy-done.3) | copy-start | bytes 6291460
  211.7 8.5 %collective-permute-start.7 = (bf16[32,4,1,512]{3,0,2,1:T(8,128)(2,1)S(1)}, bf16[32,4,1,512]{3,0,2,1:T(8,128)(2,1)S(1)}, u32[]{:S(2)}, u32[]{:S(2)}) collective-permute-start(bf16[32,4,1,512]{3,0,2,1:T(8,128)(2,1)S(1)} %slice.197), channel_id=1, source_target_pairs={{0,1},{1,2},{2,3},{3,4},{4,5},{5,6},{6,7},{7,8},{8,9},{9,10},{10,1... | collective-permute-start | bytes 393224 | tf_op jit(solution)/shard_map/ppermute | solution.py:22
  225.5 7.7 %collective-permute-start.8 = (bf16[32,4,1,512]{3,0,2,1:T(8,128)(2,1)S(1)}, bf16[32,4,1,512]{3,0,2,1:T(8,128)(2,1)S(1)}, u32[]{:S(2)}, u32[]{:S(2)}) collective-permute-start(bf16[32,4,1,512]{3,0,2,1:T(8,128)(2,1)S(1)} %slice.196), channel_id=1, source_target_pairs={{1,0},{2,1},{3,2},{4,3},{5,4},{6,5},{7,6},{8,7},{9,8},{10,9},{11,1... | collective-permute-start | bytes 393224 | tf_op jit(solution)/shard_map/ppermute | solution.py:22
  239.1 8.4 %collective-permute-start.9 = (bf16[32,4,1,512]{3,0,2,1:T(8,128)(2,1)S(1)}, bf16[32,4,1,512]{3,0,2,1:T(8,128)(2,1)S(1)}, u32[]{:S(2)}, u32[]{:S(2)}) collective-permute-start(bf16[32,4,1,512]{3,0,2,1:T(8,128)(2,1)S(1)} %slice.195), channel_id=1, source_target_pairs={{0,1},{1,2},{2,3},{3,4},{4,5},{5,6},{6,7},{7,8},{8,9},{9,10},{10,1... | collective-permute-start | bytes 393224 | tf_op jit(solution)/shard_map/ppermute | solution.py:22
  252.8 7.7 %collective-permute-start.10 = (bf16[32,4,1,512]{3,0,2,1:T(8,128)(2,1)S(1)}, bf16[32,4,1,512]{3,0,2,1:T(8,128)(2,1)S(1)}, u32[]{:S(2)}, u32[]{:S(2)}) collective-permute-start(bf16[32,4,1,512]{3,0,2,1:T(8,128)(2,1)S(1)} %slice.194), channel_id=1, source_target_pairs={{1,0},{2,1},{3,2},{4,3},{5,4},{6,5},{7,6},{8,7},{9,8},{10,9},{11,1... | collective-permute-start | bytes 393224 | tf_op jit(solution)/shard_map/ppermute | solution.py:22
  266.4 8.4 %collective-permute-start.11 = (bf16[32,4,1,512]{3,0,2,1:T(8,128)(2,1)S(1)}, bf16[32,4,1,512]{3,0,2,1:T(8,128)(2,1)S(1)}, u32[]{:S(2)}, u32[]{:S(2)}) collective-permute-start(bf16[32,4,1,512]{3,0,2,1:T(8,128)(2,1)S(1)} %slice.193), channel_id=1, source_target_pairs={{0,1},{1,2},{2,3},{3,4},{4,5},{5,6},{6,7},{7,8},{8,9},{9,10},{10,1... | collective-permute-start | bytes 393224 | tf_op jit(solution)/shard_map/ppermute | solution.py:22
  280.1 7.8 %collective-permute-start.12 = (bf16[32,4,1,512]{3,0,2,1:T(8,128)(2,1)S(1)}, bf16[32,4,1,512]{3,0,2,1:T(8,128)(2,1)S(1)}, u32[]{:S(2)}, u32[]{:S(2)}) collective-permute-start(bf16[32,4,1,512]{3,0,2,1:T(8,128)(2,1)S(1)} %slice.192), channel_id=1, source_target_pairs={{1,0},{2,1},{3,2},{4,3},{5,4},{6,5},{7,6},{8,7},{9,8},{10,9},{11,1... | collective-permute-start | bytes 393224 | tf_op jit(solution)/shard_map/ppermute | solution.py:22
  293.8 8.4 %collective-permute-start.13 = (bf16[32,4,1,512]{3,0,2,1:T(8,128)(2,1)S(1)}, bf16[32,4,1,512]{3,0,2,1:T(8,128)(2,1)S(1)}, u32[]{:S(2)}, u32[]{:S(2)}) collective-permute-start(bf16[32,4,1,512]{3,0,2,1:T(8,128)(2,1)S(1)} %slice.191), channel_id=1, source_target_pairs={{0,1},{1,2},{2,3},{3,4},{4,5},{5,6},{6,7},{7,8},{8,9},{9,10},{10,1... | collective-permute-start | bytes 393224 | tf_op jit(solution)/shard_map/ppermute | solution.py:22
  307.5 7.7 %collective-permute-start.14 = (bf16[32,4,1,512]{3,0,2,1:T(8,128)(2,1)S(1)}, bf16[32,4,1,512]{3,0,2,1:T(8,128)(2,1)S(1)}, u32[]{:S(2)}, u32[]{:S(2)}) collective-permute-start(bf16[32,4,1,512]{3,0,2,1:T(8,128)(2,1)S(1)} %slice.190), channel_id=1, source_target_pairs={{1,0},{2,1},{3,2},{4,3},{5,4},{6,5},{7,6},{8,7},{9,8},{10,9},{11,1... | collective-permute-start | bytes 393224 | tf_op jit(solution)/shard_map/ppermute | solution.py:22
  321.1 8.4 %collective-permute-start.15 = (bf16[32,4,1,512]{3,0,2,1:T(8,128)(2,1)S(1)}, bf16[32,4,1,512]{3,0,2,1:T(8,128)(2,1)S(1)}, u32[]{:S(2)}, u32[]{:S(2)}) collective-permute-start(bf16[32,4,1,512]{3,0,2,1:T(8,128)(2,1)S(1)} %slice.189), channel_id=1, source_target_pairs={{0,1},{1,2},{2,3},{3,4},{4,5},{5,6},{6,7},{7,8},{8,9},{9,10},{10,1... | collective-permute-start | bytes 393224 | tf_op jit(solution)/shard_map/ppermute | solution.py:22
  329.5 7.6 %copy-start.1 = (f32[128,64]{0,1:T(8,128)S(1)}, f32[128,64]{0,1:T(8,128)}, u32[]{:S(2)}) copy-start(f32[128,64]{0,1:T(8,128)} %param.11) | copy-start | bytes 98308
Sparse Core Ops, SparseCore 0:
  15.0 85.3 all-gather.1
